TPU v7x, 32 devices: a whole 2x2x4 slice. The times are simulated.
32 devices in a mesh: mom: 8 (over z, y), tm: 4 (over x, core).
Axes of the slice: x: 2, y: 2, z: 4, core: 2. Of those that a mesh axis runs over, the one named last changes fastest.
Arguments:
- history: float32 [4, 8, 640, 1024], P(None, 'mom', None, 'tm'), may hold values from -6 to 6
- sigma_first: float32 [4, 128, 1024], P(None, None, 'tm'), may hold values from -4 to 4
- propagator: float32 [4, 8, 384], P(None, 'mom'), may hold values from -4 to 4
Outputs:
- green_last: float32 [4, 8, 128, 1024], P(None, 'mom', None, 'tm')
- sigma_next: float32 [4, 128, 1024], P(None, None, 'tm')
All inputs are finite; a program needn't handle non-finite values.
Results may differ from a plain program's by a relative error of at most 0.0003.
Values sent between devices are 32-bit elements; how exact they have to be, the bound alone decides.
A program may use at most 64 MiB of HBM per device.

v0:
```python
import jax
import jax.numpy as jnp
from jax import lax
from jax.sharding import PartitionSpec as P


def contract(sigma, rows):
    parts = []
    for orbital in range(2):
        s_re = sigma[2 * orbital]
        s_im = sigma[2 * orbital + 1]
        h_re = rows[2 * orbital]
        h_im = rows[2 * orbital + 1]
        hp = lax.Precision.HIGHEST
        real_part = jnp.einsum("tu,kus->kts", s_re, h_re, precision=hp) - jnp.einsum(
            "tu,kus->kts", s_im, h_im, precision=hp
        )
        imag_part = jnp.einsum("tu,kus->kts", s_re, h_im, precision=hp) + jnp.einsum(
            "tu,kus->kts", s_im, h_re, precision=hp
        )
        parts.append(real_part)
        parts.append(imag_part)
    return jnp.stack(parts)


def cubic(local):
    parts = []
    for orbital in range(2):
        a_part = local[2 * orbital]
        b_part = local[2 * orbital + 1]
        parts.append(0.1 * (a_part * a_part * a_part - 3.0 * a_part * b_part * b_part))
        parts.append(0.1 * (3.0 * a_part * a_part * b_part - b_part * b_part * b_part))
    return jnp.stack(parts)


def advance(previous, convolved, factor, row_ids, col_ids, step_size):
    inner = previous + step_size * convolved
    parts = []
    for orbital in range(2):
        p_re = factor[2 * orbital][:, :, None]
        p_im = factor[2 * orbital + 1][:, :, None]
        x_re = inner[2 * orbital]
        x_im = inner[2 * orbital + 1]
        parts.append(p_re * x_re - p_im * x_im)
        parts.append(p_re * x_im + p_im * x_re)
    keep = (col_ids[None, :] <= row_ids[:, None]).astype(jnp.float32)
    return jnp.stack(parts) * keep[None, None]


def body(history, sigma_first, propagator):
    local_moms = history.shape[1]
    hist_rows = history.shape[2]
    cols = history.shape[3]
    rows_block = sigma_first.shape[1]
    new_rows = propagator.shape[2]
    blocks = new_rows // rows_block
    time_shards = lax.axis_size("tm")
    mom_shards = lax.axis_size("mom")
    total_times = cols * time_shards
    momenta = local_moms * mom_shards
    step_size = 1.0 / jnp.sqrt(jnp.float32(total_times))
    norm_factor = 1.0 / jnp.sqrt(jnp.float32(momenta))
    col_ids = lax.axis_index("tm") * cols + jnp.arange(cols, dtype=jnp.int32)
    known_ids = jnp.arange(hist_rows, dtype=jnp.int32)
    known = history * (col_ids[None, :] <= known_ids[:, None]).astype(jnp.float32)[None, None]
    buffer = jnp.concatenate(
        [known, jnp.zeros((4, local_moms, new_rows, cols), jnp.float32)], axis=2
    )
    sigma_full = lax.all_gather(sigma_first, "tm", axis=2, tiled=True)
    sigma_cols = sigma_first
    green = None
    for block in range(blocks):
        start = hist_rows + block * rows_block
        convolved = contract(sigma_full, buffer)
        previous = buffer[:, :, start - rows_block : start, :]
        row_ids = start + jnp.arange(rows_block, dtype=jnp.int32)
        factor = propagator[:, :, block * rows_block : (block + 1) * rows_block]
        green = advance(previous, convolved, factor, row_ids, col_ids, step_size)
        buffer = lax.dynamic_update_slice_in_dim(buffer, green, start, 2)
        partial_sum = jnp.sum(green, axis=1)
        last = block + 1 == blocks
        local = lax.psum(partial_sum, "mom") * norm_factor
        sigma_cols = cubic(local)
        if not last:
            sigma_full = lax.all_gather(sigma_cols, "tm", axis=2, tiled=True)
    return (green, sigma_cols)


def solution(mesh):
    placed = (P(None, "mom", None, "tm"), P(None, None, "tm"), P(None, "mom", None))
    return jax.shard_map(
        body,
        mesh=mesh,
        in_specs=placed,
        out_specs=(P(None, "mom", None, "tm"), P(None, None, "tm")),
        check_vma=False,
    )
```

profile of v0, /device:TPU:0, one launch (start us, length us, event | category | flops | bytes accessed | tf_op | source)
XLA Modules:
  0.0 359.2 jit_solution(1982264463455387781)
XLA Ops:
  7.2 0.7 all-gather.4.cloned.1.call-update
  8.0 3.2 copy.5
  11.2 0.6 slice_bitcast_fusion.71
  12.1 2.0 broadcast_multiply_fusion
  14.0 20.8 %all-gather.4.cloned.1.call-done = f32[4,128,1024]{2,1,0:T(8,128)} async-done(((f32[4,128,256]{2,1,0:T(8,128)}), f32[4,128,1024]{2,1,0:T(8,128)}) %all-gather.4.cloned.1.call-update) | async-done | bytes 2097168 | tf_op jit(solution)/shard_map/all_gather | solution.py:69
  34.9 2.2 fusion.24
  37.0 1.0 fusion.28
  38.0 1.0 fusion.30
  39.0 1.0 fusion.34
  40.0 1.0 fusion.8
  41.0 1.0 fusion.9
  42.0 1.0 fusion.10
  43.1 1.0 fusion.11
  44.2 0.8 maximum_multiply_fusion.2
  45.2 72.9 %all-reduce.5.cloned.1.call-done = f32[4,128,256]{1,2,0:T(8,128)} async-done(((f32[4,128,256]{1,2,0:T(8,128)}), f32[4,128,256]{1,2,0:T(8,128)}) %all-reduce.5.cloned.1.call-update) | async-done | bytes 524304 | tf_op jit(solution)/shard_map/psum | solution.py:82
  118.0 1.1 broadcast_multiply_fusion.3
  119.2 0.8 pad_maximum_fusion
  120.3 2.5 concatenate.62
  122.8 0.9 fusion.40
  123.7 18.3 %all-gather.6.cloned.1.call-done = f32[4,128,1024]{1,2,0:T(8,128)} async-done(((f32[4,128,256]{1,2,0:T(8,128)}), f32[4,128,1024]{1,2,0:T(8,128)}) %all-gather.6.cloned.1.call-update) | async-done | bytes 2097168 | tf_op jit(solution)/shard_map/all_gather | solution.py:85
  142.0 2.5 fusion.19
  144.5 2.4 fusion.18
  146.8 2.2 fusion.17
  149.1 2.2 fusion.16
  151.3 2.2 fusion.4
  153.5 2.2 fusion.5
  155.8 2.2 fusion.6
  158.0 2.2 fusion.7
  160.4 0.8 maximum_multiply_fusion.5
  161.3 72.9 %all-reduce.7.cloned.1.call-done = f32[4,128,256]{1,2,0:T(8,128)} async-done(((f32[4,128,256]{1,2,0:T(8,128)}), f32[4,128,256]{1,2,0:T(8,128)}) %all-reduce.7.cloned.1.call-update) | async-done | bytes 524304 | tf_op jit(solution)/shard_map/psum | solution.py:82
  234.2 1.1 broadcast_multiply_fusion.2
  235.4 0.8 pad_maximum_fusion.1
  236.2 0.3 all-reduce.9.cloned.1.call-start
  236.5 0.9 fusion.39
  237.4 20.8 %all-gather.8.cloned.1.call-done = f32[4,128,1024]{1,2,0:T(8,128)} async-done(((f32[4,128,256]{1,2,0:T(8,128)}), f32[4,128,1024]{1,2,0:T(8,128)}) %all-gather.8.cloned.1.call-update) | async-done | bytes 2097168 | tf_op jit(solution)/shard_map/all_gather | solution.py:85
  258.1 2.5 fusion.23
  260.6 2.4 fusion.22
  263.0 2.2 fusion.21
  265.2 2.2 fusion.20
  267.4 2.2 fusion
  269.7 2.2 fusion.1
  271.9 2.2 fusion.2
  274.1 2.2 fusion.3
  276.5 0.8 maximum_multiply_fusion.8
  277.4 1.0 copy.6
  278.4 71.8 %all-reduce.9.cloned.1.call-done = f32[4,128,256]{1,2,0:T(8,128)} async-done(((f32[4,128,256]{1,2,0:T(8,128)}), f32[4,128,256]{1,2,0:T(8,128)}) %all-reduce.9.cloned.1.call-update) | async-done | bytes 524304 | tf_op jit(solution)/shard_map/psum | solution.py:82
  350.1 1.1 broadcast_multiply_fusion.1
  351.4 1.0 copy.7
  (50 shorter events, 1.5 us)
Async XLA Ops:
  7.2 27.7 %all-gather.4.cloned.1.call-start = ((), (), s32[]{:S(2)}) async-start(), calls=%async_computation | async-start | bytes 2621440 | tf_op jit(solution)/shard_map/all_gather | solution.py:69
  7.9 110.1 %all-reduce.5.cloned.1.call-start = ((), (), s32[]{:S(2)}) async-start(), calls=%async_computation.1 | async-start | bytes 1048576 | tf_op jit(solution)/shard_map/psum | solution.py:82
  7.9 3.3 copy-start.3
  34.9 2.2 copy-start.2
  43.0 1.1 copy-start.8
  43.0 1.1 copy-start.9
  43.1 1.1 copy-start.10
  43.1 1.1 copy-start.11
  45.1 96.9 %all-gather.6.cloned.1.call-start = ((), (), s32[]{:S(2)}) async-start(), calls=%async_computation.2 | async-start | bytes 2621440 | tf_op jit(solution)/shard_map/all_gather | solution.py:85
  120.1 114.1 %all-reduce.7.cloned.1.call-start = ((), (), s32[]{:S(2)}) async-start(), calls=%async_computation.3 | async-start | bytes 1048576 | tf_op jit(solution)/shard_map/psum | solution.py:82
  142.0 4.9 %copy-start = (f32[4,128,1024]{1,2,0:T(8,128)S(1)}, f32[4,128,1024]{1,2,0:T(8,128)}, u32[]{:S(2)}) copy-start(f32[4,128,1024]{1,2,0:T(8,128)} %all-gather.6.cloned.1.call-done) | copy-start | bytes 6291460
  155.7 4.6 %copy-start.4 = (f32[128]{0:T(128)S(1)}, f32[128]{0:T(128)}, u32[]{:S(2)}) copy-start(f32[128]{0:T(128)} %get-tuple-element.36) | copy-start | bytes 1540
  155.7 4.6 %copy-start.5 = (f32[128]{0:T(128)S(1)}, f32[128]{0:T(128)}, u32[]{:S(2)}) copy-start(f32[128]{0:T(128)} %get-tuple-element.37) | copy-start | bytes 1540
  155.7 4.6 %copy-start.6 = (f32[128]{0:T(128)S(1)}, f32[128]{0:T(128)}, u32[]{:S(2)}) copy-start(f32[128]{0:T(128)} %get-tuple-element.38) | copy-start | bytes 1540
  155.8 4.6 %copy-start.7 = (f32[128]{0:T(128)S(1)}, f32[128]{0:T(128)}, u32[]{:S(2)}) copy-start(f32[128]{0:T(128)} %get-tuple-element.43) | copy-start | bytes 1540
  161.2 96.9 %all-gather.8.cloned.1.call-start = ((), (), s32[]{:S(2)}) async-start(), calls=%async_computation.4 | async-start | bytes 2621440 | tf_op jit(solution)/shard_map/all_gather | solution.py:85
  236.2 113.9 %all-reduce.9.cloned.1.call-start = ((), (), s32[]{:S(2)}) async-start(), calls=%async_computation.5 | async-start | bytes 1048576 | tf_op jit(solution)/shard_map/psum | solution.py:82
  258.1 4.9 %copy-start.1 = (f32[4,128,1024]{1,2,0:T(8,128)S(1)}, f32[4,128,1024]{1,2,0:T(8,128)}, u32[]{:S(2)}) copy-start(f32[4,128,1024]{1,2,0:T(8,128)} %all-gather.8.cloned.1.call-done) | copy-start | bytes 6291460
Sparse Core Ops, SparseCore 0:
  9.5 25.2 all-gather.3
  45.2 72.7 all-reduce.4
  120.2 21.7 all-gather.5
  161.4 72.7 all-reduce.6
  236.4 21.7 all-gather.7
  277.4 72.6 all-reduce.8
where the time goes:
time: 360 us; the launch traced here: 359 us
  waiting for transfers between devices  278 us (77%)
  matrix products  45.4 us (13%)
  between operations  14.5 us (4%)
  other arithmetic  12.2 us (3%)
  local copies, waits for them, and re-layouts  8.43 us (2%)
    psum x3, waiting for transfers between devices, body(): local = lax.psum(partial_sum, 'mom') * norm_factor  217 us
    all_gather x2, waiting for transfers between devices, body(): sigma_full = lax.all_gather(sigma_cols, 'tm', axis=2, tiled=True)  39 us
    all_gather x1, waiting for transfers between devices, body(): sigma_full = lax.all_gather(sigma_first, 'tm', axis=2, tiled=True)  20.8 us
    dot_general x6, matrix products, contract(): jnp.einsum('tu,kus->kts', s_re, h_im, precision=hp)  12.6 us
    dot_general x6, matrix products, contract(): jnp.einsum('tu,kus->kts', s_re, h_re, precision=hp)  11.1 us
    dot_general x6, matrix products, contract(): jnp.einsum('tu,kus->kts', s_im, h_re, precision=hp)  10.9 us
    dot_general x6, matrix products, contract(): jnp.einsum('tu,kus->kts', s_im, h_im, precision=hp)  10.8 us
  transfers between devices with their start and end apart: 6, of which 6 were waited for; matrix products, arithmetic and copies ran while one was open for 3% of the time, Pallas kernels for 0%

commit v1 on v0

--- a/solution.py
+++ b/solution.py
@@ -1,7 +1,16 @@
+import functools
+import math
+
 import jax
 import jax.numpy as jnp
 from jax import lax
+from jax.experimental import pallas as pl
+from jax.experimental.pallas import tpu as pltpu
 from jax.sharding import PartitionSpec as P
+
+MESH = pl.DeviceIdType.MESH
+PAIR = 2
+SUBLANES = 8
 
 
 def contract(sigma, rows):
@@ -23,14 +32,15 @@
     return jnp.stack(parts)
 
 
+def cubic_pair(a_part, b_part):
+    return (
+        0.1 * (a_part * a_part * a_part - 3.0 * a_part * b_part * b_part),
+        0.1 * (3.0 * a_part * a_part * b_part - b_part * b_part * b_part),
+    )
+
+
 def cubic(local):
-    parts = []
-    for orbital in range(2):
-        a_part = local[2 * orbital]
-        b_part = local[2 * orbital + 1]
-        parts.append(0.1 * (a_part * a_part * a_part - 3.0 * a_part * b_part * b_part))
-        parts.append(0.1 * (3.0 * a_part * a_part * b_part - b_part * b_part * b_part))
-    return jnp.stack(parts)
+    return jnp.stack(cubic_pair(local[0], local[1]) + cubic_pair(local[2], local[3]))
 
 
 def advance(previous, convolved, factor, row_ids, col_ids, step_size):
@@ -47,7 +57,7 @@
     return jnp.stack(parts) * keep[None, None]
 
 
-def body(history, sigma_first, propagator):
+def plain_body(history, sigma_first, propagator):
     local_moms = history.shape[1]
     hist_rows = history.shape[2]
     cols = history.shape[3]
@@ -56,20 +66,18 @@
     blocks = new_rows // rows_block
     time_shards = lax.axis_size("tm")
     mom_shards = lax.axis_size("mom")
-    total_times = cols * time_shards
-    momenta = local_moms * mom_shards
-    step_size = 1.0 / jnp.sqrt(jnp.float32(total_times))
-    norm_factor = 1.0 / jnp.sqrt(jnp.float32(momenta))
+    step_size = 1.0 / jnp.sqrt(jnp.float32(cols * time_shards))
+    norm_factor = 1.0 / jnp.sqrt(jnp.float32(local_moms * mom_shards))
     col_ids = lax.axis_index("tm") * cols + jnp.arange(cols, dtype=jnp.int32)
     known_ids = jnp.arange(hist_rows, dtype=jnp.int32)
     known = history * (col_ids[None, :] <= known_ids[:, None]).astype(jnp.float32)[None, None]
     buffer = jnp.concatenate(
         [known, jnp.zeros((4, local_moms, new_rows, cols), jnp.float32)], axis=2
     )
-    sigma_full = lax.all_gather(sigma_first, "tm", axis=2, tiled=True)
     sigma_cols = sigma_first
     green = None
     for block in range(blocks):
+        sigma_full = lax.all_gather(sigma_cols, "tm", axis=2, tiled=True)
         start = hist_rows + block * rows_block
         convolved = contract(sigma_full, buffer)
         previous = buffer[:, :, start - rows_block : start, :]
@@ -77,13 +85,293 @@
         factor = propagator[:, :, block * rows_block : (block + 1) * rows_block]
         green = advance(previous, convolved, factor, row_ids, col_ids, step_size)
         buffer = lax.dynamic_update_slice_in_dim(buffer, green, start, 2)
-        partial_sum = jnp.sum(green, axis=1)
-        last = block + 1 == blocks
-        local = lax.psum(partial_sum, "mom") * norm_factor
+        local = lax.psum(jnp.sum(green, axis=1), "mom") * norm_factor
         sigma_cols = cubic(local)
-        if not last:
-            sigma_full = lax.all_gather(sigma_cols, "tm", axis=2, tiled=True)
     return (green, sigma_cols)
+
+
+def split(x):
+    high = x.astype(jnp.bfloat16)
+    return high, (x - high.astype(jnp.float32)).astype(jnp.bfloat16)
+
+
+def window_kernel(
+    moms, shards,
+    hist_ref, sig_ref, prop_ref, green_ref, next_ref,
+    hist32, gh, gl, gcur, ybuf, part, zbuf, s32, conv,
+    load_sem, ys, yr, zs, zr, gzs, gzr, gys, gyr, ts, tr,
+):
+    orbitals, _, hist_rows, cols = hist_ref.shape
+    rows = sig_ref.shape[2]
+    blocks = prop_ref.shape[0] // rows
+    outer = moms // PAIR
+    half = rows // PAIR
+    piece = half // outer
+    dt = 1.0 / math.sqrt(cols * shards)
+    norm = 1.0 / math.sqrt(moms)
+    mom = lax.axis_index("mom")
+    tm = lax.axis_index("tm")
+    y = lax.rem(mom, PAIR)
+    z = lax.div(mom, PAIR)
+    partner = z * PAIR + (1 - y)
+    peers = [lax.rem(z + d, outer) * PAIR + y for d in range(1, outer)]
+
+    loads = [pltpu.make_async_copy(sig_ref, s32.at[0, :, tm], load_sem.at[0])]
+    loads += [
+        pltpu.make_async_copy(hist_ref.at[o], hist32.at[o], load_sem.at[1 + o]) for o in range(orbitals)
+    ]
+    for load in loads:
+        load.start()
+
+    barrier = pltpu.get_barrier_semaphore()
+    pl.semaphore_signal(barrier, inc=1, device_id=(partner, tm), device_id_type=MESH)
+    for peer in peers:
+        pl.semaphore_signal(barrier, inc=1, device_id=(peer, tm), device_id_type=MESH)
+    for d in range(1, shards):
+        pl.semaphore_signal(
+            barrier, inc=1, device_id=(mom, lax.rem(tm + d, shards)), device_id_type=MESH
+        )
+    pl.semaphore_wait(barrier, 1 + len(peers) + shards - 1)
+
+    def width(b, shard):
+        return max(0, min(cols, hist_rows + b * rows - shard * cols))
+
+    def share(b, o, src, dst):
+        view = s32.at[b, o, src, :, :, pl.ds(0, width(b, src))]
+        return pltpu.make_async_remote_copy(
+            src_ref=view, dst_ref=view, send_sem=ts.at[b, o, dst], recv_sem=tr.at[b, o, src],
+            device_id=(mom, jnp.int32(dst)), device_id_type=MESH,
+        )
+
+    def spread(b, o):
+        for src in range(1, shards):
+            if width(b, src):
+                @pl.when(tm == src)
+                def _():
+                    for dst in range(src):
+                        share(b, o, src, dst).start()
+
+    half_mine = pl.ds(pl.multiple_of(y * half, half), half)
+    half_other = pl.ds(pl.multiple_of((1 - y) * half, half), half)
+    own = pl.ds(pl.multiple_of(y * half + z * piece, piece), piece)
+
+    def pair_sum(b, o):
+        return pltpu.make_async_remote_copy(
+            src_ref=gcur.at[b, o, :, half_other], dst_ref=ybuf.at[b, o],
+            send_sem=ys.at[b, o], recv_sem=yr.at[b, o],
+            device_id=(partner, tm), device_id_type=MESH,
+        )
+
+    def line_sum(b, o, d):
+        target = lax.rem(z + d, outer)
+        return pltpu.make_async_remote_copy(
+            src_ref=part.at[b, o, :, pl.ds(pl.multiple_of(target * piece, piece), piece)],
+            dst_ref=zbuf.at[b, o, d - 1],
+            send_sem=zs.at[b, o, d - 1], recv_sem=zr.at[b, o, d - 1],
+            device_id=(peers[d - 1], tm), device_id_type=MESH,
+        )
+
+    def line_copy(b, o, d):
+        view = s32.at[b + 1, o, tm, :, own]
+        return pltpu.make_async_remote_copy(
+            src_ref=view, dst_ref=view,
+            send_sem=gzs.at[b, o, d - 1], recv_sem=gzr.at[b, o, d - 1],
+            device_id=(peers[d - 1], tm), device_id_type=MESH,
+        )
+
+    def pair_copy(b, o):
+        view = s32.at[b + 1, o, tm, :, half_mine]
+        return pltpu.make_async_remote_copy(
+            src_ref=view, dst_ref=view, send_sem=gys.at[b, o], recv_sem=gyr.at[b, o],
+            device_id=(partner, tm), device_id_type=MESH,
+        )
+
+    loads[0].wait()
+    for o in range(orbitals):
+        spread(0, o)
+
+    col_ids = tm * cols + lax.broadcasted_iota(jnp.int32, (rows, cols), 1)
+    row_iota = lax.broadcasted_iota(jnp.int32, (rows, cols), 0)
+    for o in range(orbitals):
+        loads[1 + o].wait()
+        for r in range(0, hist_rows, rows):
+            for c in range(2):
+                x = jnp.where(col_ids <= row_iota + r, hist32[o, c, r : r + rows], 0.0)
+                high, low = split(x)
+                gh[o, c, r : r + rows] = high
+                gl[o, c, r : r + rows] = low
+
+    for b in range(blocks):
+        start = hist_rows + b * rows
+        last = b + 1 == blocks
+        keep = col_ids <= row_iota + start
+        active = tm * cols < start + rows
+
+        for o in range(orbitals):
+            conv[o] = jnp.zeros((2, rows, cols), jnp.float32)
+            for shard in range(shards):
+                depth = width(b, shard)
+                if not depth:
+                    continue
+
+                @pl.when(tm < shard)
+                def _():
+                    share(b, o, shard, 0).wait_recv()
+
+                @pl.when(tm <= shard)
+                def _():
+                    re_high, re_low = split(s32[b, o, shard, 0, :, 0:depth])
+                    im_high, im_low = split(s32[b, o, shard, 1, :, 0:depth])
+                    lhs_high = jnp.concatenate([re_high, im_high], axis=0)
+                    lhs_both = jnp.concatenate([re_high, im_high, re_low, im_low], axis=0)
+                    u = shard * cols
+                    totals = []
+                    for c in range(2):
+                        main = jnp.dot(
+                            lhs_both, gh[o, c, u : u + depth], preferred_element_type=jnp.float32
+                        )
+                        rest = jnp.dot(
+                            lhs_high, gl[o, c, u : u + depth], preferred_element_type=jnp.float32
+                        )
+                        totals.append(main[: 2 * rows] + (main[2 * rows :] + rest))
+                    conv[o, 0] += totals[0][:rows] - totals[1][rows:]
+                    conv[o, 1] += totals[1][:rows] + totals[0][rows:]
+
+            p_re = prop_ref[b * rows : (b + 1) * rows, 2 * o : 2 * o + 1]
+            p_im = prop_ref[b * rows : (b + 1) * rows, 2 * o + 1 : 2 * o + 2]
+            if b == 0:
+                before = hist_rows - rows
+                seen = col_ids <= row_iota + before
+                prev = [jnp.where(seen, hist32[o, c, before:hist_rows], 0.0) for c in range(2)]
+            else:
+                prev = [gcur[b - 1, o, c] for c in range(2)]
+            x_re = prev[0] + dt * conv[o, 0]
+            x_im = prev[1] + dt * conv[o, 1]
+            new = [
+                jnp.where(keep, p_re * x_re - p_im * x_im, 0.0),
+                jnp.where(keep, p_re * x_im + p_im * x_re, 0.0),
+            ]
+            for c in range(2):
+                gcur[b, o, c] = new[c]
+
+            @pl.when(active)
+            def _():
+                pair_sum(b, o).start()
+
+            for c in range(2):
+                if last:
+                    green_ref[o, c] = new[c]
+                else:
+                    high, low = split(new[c])
+                    gh[o, c, start : start + rows] = high
+                    gl[o, c, start : start + rows] = low
+
+        @pl.when(active)
+        def _():
+            for o in range(orbitals):
+                pair_sum(b, o).wait_recv()
+                part[b, o] = gcur[b, o, :, half_mine] + ybuf[b, o]
+                for d in range(1, outer):
+                    line_sum(b, o, d).start()
+            for o in range(orbitals):
+                total = part[b, o, :, pl.ds(pl.multiple_of(z * piece, piece), piece)]
+                for d in range(1, outer):
+                    line_sum(b, o, d).wait_recv()
+                    total = total + zbuf[b, o, d - 1]
+                total = total * norm
+                s_re, s_im = cubic_pair(total[0], total[1])
+                s32[b + 1, o, tm, 0, own] = s_re
+                s32[b + 1, o, tm, 1, own] = s_im
+                for d in range(1, outer):
+                    line_copy(b, o, d).start()
+            for o in range(orbitals):
+                for d in range(1, outer):
+                    line_copy(b, o, d).wait_recv()
+                pair_copy(b, o).start()
+            for o in range(orbitals):
+                pair_copy(b, o).wait_recv()
+                if not last:
+                    spread(b + 1, o)
+
+    for o in range(orbitals):
+        next_ref[o] = s32[blocks, o, tm]
+
+    for b in range(blocks):
+        for o in range(orbitals):
+            for src in range(1, shards):
+                if width(b, src):
+                    @pl.when(tm == src)
+                    def _():
+                        for dst in range(src):
+                            share(b, o, src, dst).wait_send()
+
+        @pl.when(tm * cols < hist_rows + (b + 1) * rows)
+        def _():
+            for o in range(orbitals):
+                pair_sum(b, o).wait_send()
+                pair_copy(b, o).wait_send()
+                for d in range(1, outer):
+                    line_sum(b, o, d).wait_send()
+                    line_copy(b, o, d).wait_send()
+
+
+def kernel_body(moms, shards, history, sigma_first, propagator):
+    comps, _, hist_rows, cols = history.shape
+    rows = sigma_first.shape[1]
+    new_rows = propagator.shape[2]
+    blocks = new_rows // rows
+    orbitals = comps // 2
+    outer = moms // PAIR
+    half = rows // PAIR
+    piece = half // outer
+    f32, bf16 = jnp.float32, jnp.bfloat16
+    dma = pltpu.SemaphoreType.DMA
+    vmem = pl.BlockSpec(memory_space=pltpu.VMEM)
+    hbm = pl.BlockSpec(memory_space=pl.ANY)
+    line = (blocks, orbitals, max(outer - 1, 1))
+    green, sigma = pl.pallas_call(
+        functools.partial(window_kernel, moms, shards),
+        out_shape=(
+            jax.ShapeDtypeStruct((orbitals, 2, rows, cols), f32),
+            jax.ShapeDtypeStruct((orbitals, 2, rows, cols), f32),
+        ),
+        in_specs=[hbm, hbm, vmem],
+        out_specs=(vmem, vmem),
+        scratch_shapes=[
+            pltpu.VMEM((orbitals, 2, hist_rows, cols), f32),
+            pltpu.VMEM((orbitals, 2, hist_rows + new_rows, cols), bf16),
+            pltpu.VMEM((orbitals, 2, hist_rows + new_rows, cols), bf16),
+            pltpu.VMEM((blocks, orbitals, 2, rows, cols), f32),
+            pltpu.VMEM((blocks, orbitals, 2, half, cols), f32),
+            pltpu.VMEM((blocks, orbitals, 2, half, cols), f32),
+            pltpu.VMEM(line + (2, piece, cols), f32),
+            pltpu.VMEM((blocks + 1, orbitals, shards, 2, rows, cols), f32),
+            pltpu.VMEM((orbitals, 2, rows, cols), f32),
+            dma((1 + orbitals,)),
+            dma((blocks, orbitals)), dma((blocks, orbitals)),
+            dma(line), dma(line), dma(line), dma(line),
+            dma((blocks, orbitals)), dma((blocks, orbitals)),
+            dma((blocks, orbitals, shards)), dma((blocks, orbitals, shards)),
+        ],
+        compiler_params=pltpu.CompilerParams(
+            collective_id=0, has_side_effects=True, vmem_limit_bytes=56 * 1024 * 1024
+        ),
+    )(
+        history.reshape(orbitals, 2, hist_rows, cols),
+        sigma_first.reshape(orbitals, 2, rows, cols),
+        propagator.reshape(comps, new_rows).T,
+    )
+    return green.reshape(comps, 1, rows, cols), sigma.reshape(comps, rows, cols)
+
+
+def body(history, sigma_first, propagator):
+    moms, shards = lax.axis_size("mom"), lax.axis_size("tm")
+    rows = sigma_first.shape[1]
+    tiled = moms % PAIR == 0 and rows % (moms * SUBLANES) == 0
+    whole = history.shape[2] + propagator.shape[2] == history.shape[3] * shards
+    if history.shape[1] == 1 and tiled and whole:
+        return kernel_body(moms, shards, history, sigma_first, propagator)
+    return plain_body(history, sigma_first, propagator)
 
 
 def solution(mesh):

time: 360 us -> 92.3 us (0.26)
  waiting for transfers between devices: 278 us -> 0 us
  Pallas kernels: 0 us -> 86.1 us
  matrix products: 45.4 us -> 0 us
  between operations: 14.5 us -> 0.64 us
  other arithmetic: 12.2 us -> 0 us
    psum x3 -> x0, waiting for transfers between devices: 217 us -> none  [body(): local = lax.psum(partial_sum, 'mom') * norm_factor]
    pallas_call x0 -> x1, Pallas kernels: none -> 86.1 us  [kernel_body(): pl.pallas_call(functools.partial(window_kernel, moms, shards), out_shape=...]
    all_gather x3 -> x0, waiting for transfers between devices: 59.8 us -> none  [the longest x2 39 us: body(): sigma_full = lax.all_gather(sigma_cols, 'tm', axis=2, tiled=True)]
    dot_general x24 -> x0, matrix products: 45.4 us -> none  [the longest x6 12.6 us: contract(): jnp.einsum('tu,kus->kts', s_re, h_im, precision=hp)]
    mul x11 -> x0, other arithmetic: 8.14 us -> none  [the longest x3 3.26 us: body(): local = lax.psum(partial_sum, 'mom') * norm_factor]
  transfers between devices with their start and end apart: 6 -> 0, of which waited for: 6 -> 0; matrix products, arithmetic and copies ran while one was open for 3% -> 0% of each run, Pallas kernels for 0% -> 0%
where the time goes in v1:
time: 92.3 us; the launch traced here: 92 us
  Pallas kernels  86.1 us (93%)
  local copies, waits for them, and re-layouts  5.25 us (6%)
    pallas_call x1, Pallas kernels, kernel_body(): pl.pallas_call(functools.partial(window_kernel, moms, shards), out_shape=...  86.1 us
    unnamed x3, local copies, waits for them, and re-layouts  5.25 us

profile of v1, /device:TPU:0, one launch (start us, length us, event | category | flops | bytes accessed | tf_op | source)
XLA Modules:
  0.0 92.0 jit_solution(16461625497400294575)
XLA Ops:
  0.6 1.5 %copy.5 = f32[4,1,384]{0,2,1:T(8,128)} copy(f32[4,1,384]{2,1,0:T(1,128)} %param.5) | data formatting | bytes 12288 | tf_op args[2]
  2.1 86.1 %shard_map.50 = (f32[2,2,128,256]{3,2,1,0:T(8,128)}, f32[2,2,128,256]{3,2,1,0:T(8,128)}) custom-call(f32[2,2,640,256]{3,2,1,0:T(8,128)} %bitcast.9, f32[2,2,128,256]{3,2,1,0:T(8,128)} %bitcast.11, f32[384,4]{1,0:T(8,128)} %bitcast.10), custom_call_target="tpu_custom_call" | custom-call | tf_op jit(solution)/shard_map/pallas_call | solution.py:332
  88.3 1.9 %copy.9 = f32[4,1,128,256]{3,2,1,0:T(8,128)} copy(f32[4,1,128,256]{3,2,1,0:T(8,128)} %bitcast.13) | data formatting | bytes 1048576
  90.1 1.9 %copy.10 = f32[4,128,256]{2,1,0:T(8,128)} copy(f32[4,128,256]{2,1,0:T(8,128)} %bitcast.12) | data formatting | bytes 1048576

commit v2 on v0

v2 whole, which is shorter than its diff:
```python
import functools
import math

import jax
import jax.numpy as jnp
from jax import lax
from jax.experimental import pallas as pl
from jax.experimental.pallas import tpu as pltpu
from jax.sharding import PartitionSpec as P

MESH = pl.DeviceIdType.MESH
PAIR = 2
SUBLANES = 8
LANES = 128
CHUNKS = 2


def contract(sigma, rows):
    parts = []
    for orbital in range(2):
        s_re = sigma[2 * orbital]
        s_im = sigma[2 * orbital + 1]
        h_re = rows[2 * orbital]
        h_im = rows[2 * orbital + 1]
        hp = lax.Precision.HIGHEST
        real_part = jnp.einsum("tu,kus->kts", s_re, h_re, precision=hp) - jnp.einsum(
            "tu,kus->kts", s_im, h_im, precision=hp
        )
        imag_part = jnp.einsum("tu,kus->kts", s_re, h_im, precision=hp) + jnp.einsum(
            "tu,kus->kts", s_im, h_re, precision=hp
        )
        parts.append(real_part)
        parts.append(imag_part)
    return jnp.stack(parts)


def cubic_pair(a_part, b_part):
    return (
        0.1 * (a_part * a_part * a_part - 3.0 * a_part * b_part * b_part),
        0.1 * (3.0 * a_part * a_part * b_part - b_part * b_part * b_part),
    )


def cubic(local):
    return jnp.stack(cubic_pair(local[0], local[1]) + cubic_pair(local[2], local[3]))


def advance(previous, convolved, factor, row_ids, col_ids, step_size):
    inner = previous + step_size * convolved
    parts = []
    for orbital in range(2):
        p_re = factor[2 * orbital][:, :, None]
        p_im = factor[2 * orbital + 1][:, :, None]
        x_re = inner[2 * orbital]
        x_im = inner[2 * orbital + 1]
        parts.append(p_re * x_re - p_im * x_im)
        parts.append(p_re * x_im + p_im * x_re)
    keep = (col_ids[None, :] <= row_ids[:, None]).astype(jnp.float32)
    return jnp.stack(parts) * keep[None, None]


def plain_body(history, sigma_first, propagator):
    local_moms = history.shape[1]
    hist_rows = history.shape[2]
    cols = history.shape[3]
    rows_block = sigma_first.shape[1]
    new_rows = propagator.shape[2]
    blocks = new_rows // rows_block
    time_shards = lax.axis_size("tm")
    mom_shards = lax.axis_size("mom")
    step_size = 1.0 / jnp.sqrt(jnp.float32(cols * time_shards))
    norm_factor = 1.0 / jnp.sqrt(jnp.float32(local_moms * mom_shards))
    col_ids = lax.axis_index("tm") * cols + jnp.arange(cols, dtype=jnp.int32)
    known_ids = jnp.arange(hist_rows, dtype=jnp.int32)
    known = history * (col_ids[None, :] <= known_ids[:, None]).astype(jnp.float32)[None, None]
    buffer = jnp.concatenate(
        [known, jnp.zeros((4, local_moms, new_rows, cols), jnp.float32)], axis=2
    )
    sigma_cols = sigma_first
    green = None
    for block in range(blocks):
        sigma_full = lax.all_gather(sigma_cols, "tm", axis=2, tiled=True)
        start = hist_rows + block * rows_block
        convolved = contract(sigma_full, buffer)
        previous = buffer[:, :, start - rows_block : start, :]
        row_ids = start + jnp.arange(rows_block, dtype=jnp.int32)
        factor = propagator[:, :, block * rows_block : (block + 1) * rows_block]
        green = advance(previous, convolved, factor, row_ids, col_ids, step_size)
        buffer = lax.dynamic_update_slice_in_dim(buffer, green, start, 2)
        local = lax.psum(jnp.sum(green, axis=1), "mom") * norm_factor
        sigma_cols = cubic(local)
    return (green, sigma_cols)


def split(x):
    high = x.astype(jnp.bfloat16)
    return high, (x - high.astype(jnp.float32)).astype(jnp.bfloat16)


def stage_order(blocks, tasks, last_stage):
    lag = (3.0, 4.0, 4.0, 3.0, 3.0, 1.5)
    busy = (1.0, 0.2, 0.2, 0.1, 0.1, 0.1)
    ready = [(0.0, 0, task, 0) for task in range(tasks)]
    now, order = 0.0, []
    while ready:
        item = min(ready)
        ready.remove(item)
        when, block, task, stage = item
        order.append((stage, block, task))
        now = max(now, when) + busy[stage]
        done = now + lag[stage]
        final = block + 1 == blocks
        if stage < last_stage and not (final and stage == 4):
            ready.append((done, block, task, stage + 1))
        elif not final:
            ready.append((done, block + 1, task, 0))
    return order


def window_kernel(
    moms, shards, chunks,
    hist_ref, sig_ref, prop_ref, green_ref, next_ref,
    hist32, gh, gl, gcur, ybuf, part, zbuf, s32, conv, pcol,
    load_sem, ys, yr, zs, zr, gzs, gzr, gys, gyr, ts, tr, fs, fr,
):
    orbitals, _, hist_rows, cols = hist_ref.shape
    rows = sig_ref.shape[2]
    blocks = prop_ref.shape[1] // rows
    outer = moms // PAIR
    w = rows // chunks
    half = cols // PAIR
    piece = w // outer
    dt = 1.0 / math.sqrt(cols * shards)
    norm = 1.0 / math.sqrt(moms)
    mom = lax.axis_index("mom")
    tm = lax.axis_index("tm")
    y = lax.rem(mom, PAIR)
    z = lax.div(mom, PAIR)
    partner = z * PAIR + (1 - y)
    peers = [lax.rem(z + d, outer) * PAIR + y for d in range(1, outer)]
    place = lax.rem(tm, PAIR)
    twin = tm + 1 - 2 * place

    loads = [pltpu.make_async_copy(sig_ref, s32.at[0, :, tm], load_sem.at[0])]
    loads += [
        pltpu.make_async_copy(hist_ref.at[o], hist32.at[o], load_sem.at[1 + o]) for o in range(orbitals)
    ]
    for load in loads:
        load.start()

    barrier = pltpu.get_barrier_semaphore()
    pl.semaphore_signal(barrier, inc=1, device_id=(partner, tm), device_id_type=MESH)
    for peer in peers:
        pl.semaphore_signal(barrier, inc=1, device_id=(peer, tm), device_id_type=MESH)
    for d in range(1, shards):
        pl.semaphore_signal(
            barrier, inc=1, device_id=(mom, lax.rem(tm + d, shards)), device_id_type=MESH
        )
    pl.semaphore_wait(barrier, 1 + len(peers) + shards - 1)

    def width(b, shard):
        return max(0, min(cols, hist_rows + b * rows - shard * cols))

    def remote(src, dst, send, recv, device):
        return pltpu.make_async_remote_copy(
            src_ref=src, dst_ref=dst, send_sem=send, recv_sem=recv,
            device_id=device, device_id_type=MESH,
        )

    def chunk(r):
        return pl.ds(r * w, w)

    def near(b, r, o, src):
        view = s32.at[b, o, src, :, chunk(r), pl.ds(0, width(b, src))]
        return remote(view, view, ts.at[b, r, o, 0], tr.at[b, r, o, src], (mom, jnp.int32(src - 1)))

    def far(b, r, o, src, dst):
        view = s32.at[b, o, src, dst % PAIR, chunk(r), pl.ds(0, width(b, src))]
        return remote(view, view, ts.at[b, r, o, 1 + dst], tr.at[b, r, o, src], (mom, jnp.int32(dst)))

    def passed(b, r, o, src, component):
        view = s32.at[b, o, src, component, chunk(r), pl.ds(0, width(b, src))]
        return remote(view, view, fs.at[b, r, o, src], fr.at[b, r, o, src], (mom, twin))

    def spread(b, r, o, act):
        for src in range(1, shards):
            base = src - src % PAIR
            if width(b, src):
                @pl.when(tm == src)
                def _():
                    for dst in range(base):
                        act(far(b, r, o, src, dst))
                    if src % PAIR:
                        act(near(b, r, o, src))

    def forward(b, r, o, go):
        for src in range(PAIR, shards):
            base = src - src % PAIR
            if width(b, src):
                @pl.when(tm < base)
                def _():
                    if go:
                        far(b, r, o, src, 0).wait_recv()
                        passed(b, r, o, src, place).start()
                    else:
                        passed(b, r, o, src, place).wait_send()

    half_mine = pl.ds(pl.multiple_of(y * half, LANES), half)
    half_other = pl.ds(pl.multiple_of((1 - y) * half, LANES), half)

    def strip(r, k):
        return pl.ds(pl.multiple_of(r * w + k * piece, SUBLANES), piece)

    def pair_sum(b, r, o):
        return remote(
            gcur.at[b, o, :, chunk(r), half_other], ybuf.at[b, r, o],
            ys.at[b, r, o], yr.at[b, r, o], (partner, tm),
        )

    def line_sum(b, r, o, d):
        target = lax.rem(z + d, outer)
        return remote(
            part.at[b, o, :, strip(r, target)], zbuf.at[b, r, o, d - 1],
            zs.at[b, r, o, d - 1], zr.at[b, r, o, d - 1], (peers[d - 1], tm),
        )

    def line_copy(b, r, o, d):
        view = s32.at[b + 1, o, tm, :, strip(r, z), half_mine]
        return remote(view, view, gzs.at[b, r, o, d - 1], gzr.at[b, r, o, d - 1], (peers[d - 1], tm))

    def pair_copy(b, r, o):
        view = s32.at[b + 1, o, tm, :, chunk(r), half_mine]
        return remote(view, view, gys.at[b, r, o], gyr.at[b, r, o], (partner, tm))

    tasks = [(r, o) for r in range(chunks) for o in range(orbitals)]
    start_copy = lambda copy: copy.start()
    loads[0].wait()
    for r, o in tasks:
        spread(0, r, o, start_copy)

    col_ids = tm * cols + lax.broadcasted_iota(jnp.int32, (rows, cols), 1)
    row_iota = lax.broadcasted_iota(jnp.int32, (rows, cols), 0)
    keep_cols = tm * cols + lax.broadcasted_iota(jnp.int32, (w, cols), 1)
    keep_rows = lax.broadcasted_iota(jnp.int32, (w, cols), 0)
    square = lax.broadcasted_iota(jnp.int32, (rows, rows), 0)
    diagonal = square == lax.broadcasted_iota(jnp.int32, (rows, rows), 1)
    for b in range(blocks):
        for c in range(2 * orbitals):
            line = prop_ref[c : c + 1, b * rows : (b + 1) * rows]
            pcol[b, c] = jnp.sum(jnp.where(diagonal, line, 0.0), axis=1, keepdims=True)
    gh[:, :, hist_rows:] = jnp.zeros((orbitals, 2, blocks * rows, cols), jnp.bfloat16)
    gl[:, :, hist_rows:] = jnp.zeros((orbitals, 2, blocks * rows, cols), jnp.bfloat16)
    for o in range(orbitals):
        loads[1 + o].wait()
        for r in range(0, hist_rows, rows):
            for c in range(2):
                x = jnp.where(col_ids <= row_iota + r, hist32[o, c, r : r + rows], 0.0)
                high, low = split(x)
                gh[o, c, r : r + rows] = high
                gl[o, c, r : r + rows] = low
    for r, o in tasks:
        forward(0, r, o, True)

    def compute(b, r, o):
        start = hist_rows + b * rows + r * w
        span = slice(r * w, (r + 1) * w)
        conv[...] = jnp.zeros(conv.shape, jnp.float32)
        for shard in range(shards):
            depth = width(b, shard)
            if not depth:
                continue
            base = shard - shard % PAIR
            if shard % PAIR:
                @pl.when(tm == base)
                def _():
                    near(b, r, o, shard).wait_recv()
            if base:
                @pl.when(tm < base)
                def _():
                    passed(b, r, o, shard, 0).wait_recv()

            @pl.when(tm <= shard)
            def _():
                re_high, re_low = split(s32[b, o, shard, 0, span, 0:depth])
                im_high, im_low = split(s32[b, o, shard, 1, span, 0:depth])
                lhs_high = jnp.concatenate([re_high, im_high], axis=0)
                lhs_both = jnp.concatenate([re_high, im_high, re_low, im_low], axis=0)
                u = shard * cols
                totals = []
                for c in range(2):
                    main = jnp.dot(
                        lhs_both, gh[o, c, u : u + depth], preferred_element_type=jnp.float32
                    )
                    rest = jnp.dot(
                        lhs_high, gl[o, c, u : u + depth], preferred_element_type=jnp.float32
                    )
                    totals.append(main[: 2 * w] + (main[2 * w :] + rest))
                conv[0] += totals[0][:w] - totals[1][w:]
                conv[1] += totals[1][:w] + totals[0][w:]

        p_re = pcol[b, 2 * o, span]
        p_im = pcol[b, 2 * o + 1, span]
        if b == 0:
            before = start - rows
            seen = keep_cols <= keep_rows + before
            prev = [jnp.where(seen, hist32[o, c, before : before + w], 0.0) for c in range(2)]
        else:
            prev = [gcur[b - 1, o, c, span] for c in range(2)]
        x_re = prev[0] + dt * conv[0]
        x_im = prev[1] + dt * conv[1]
        keep = keep_cols <= keep_rows + start
        new = [
            jnp.where(keep, p_re * x_re - p_im * x_im, 0.0),
            jnp.where(keep, p_re * x_im + p_im * x_re, 0.0),
        ]
        for c in range(2):
            gcur[b, o, c, span] = new[c]

        @pl.when(active(b))
        def _():
            pair_sum(b, r, o).start()

        for c in range(2):
            if b + 1 == blocks:
                green_ref[o, c, span] = new[c]
            else:
                high, low = split(new[c])
                gh[o, c, start : start + w] = high
                gl[o, c, start : start + w] = low

    def active(b):
        return tm * cols < hist_rows + (b + 1) * rows

    def sum_pair(b, r, o):
        pair_sum(b, r, o).wait_recv()
        part[b, o, :, chunk(r)] = gcur[b, o, :, chunk(r), half_mine] + ybuf[b, r, o]
        for d in range(1, outer):
            line_sum(b, r, o, d).start()

    def sum_line(b, r, o):
        total = part[b, o, :, strip(r, z)]
        for d in range(1, outer):
            line_sum(b, r, o, d).wait_recv()
            total = total + zbuf[b, r, o, d - 1]
        total = total * norm
        s_re, s_im = cubic_pair(total[0], total[1])
        s32[b + 1, o, tm, 0, strip(r, z), half_mine] = s_re
        s32[b + 1, o, tm, 1, strip(r, z), half_mine] = s_im
        for d in range(1, outer):
            line_copy(b, r, o, d).start()

    def copy_line(b, r, o):
        for d in range(1, outer):
            line_copy(b, r, o, d).wait_recv()
        pair_copy(b, r, o).start()

    def copy_pair(b, r, o):
        pair_copy(b, r, o).wait_recv()
        if b + 1 == blocks:
            next_ref[o, :, chunk(r)] = s32[blocks, o, tm, :, chunk(r)]
        else:
            spread(b + 1, r, o, start_copy)

    stages = (compute, sum_pair, sum_line, copy_line, copy_pair)
    for stage, b, task in stage_order(blocks, len(tasks), 5):
        r, o = tasks[task]
        if stage == 0:
            compute(b, r, o)
        elif stage == 5:
            forward(b + 1, r, o, True)
        else:
            @pl.when(active(b))
            def _():
                stages[stage](b, r, o)

    for b in range(blocks):
        for r, o in tasks:
            spread(b, r, o, lambda copy: copy.wait_send())
            forward(b, r, o, False)

            @pl.when(active(b))
            def _():
                pair_sum(b, r, o).wait_send()
                pair_copy(b, r, o).wait_send()
                for d in range(1, outer):
                    line_sum(b, r, o, d).wait_send()
                    line_copy(b, r, o, d).wait_send()


def kernel_body(moms, shards, history, sigma_first, propagator):
    comps, _, hist_rows, cols = history.shape
    rows = sigma_first.shape[1]
    new_rows = propagator.shape[2]
    blocks = new_rows // rows
    orbitals = comps // 2
    outer = moms // PAIR
    w = rows // CHUNKS
    half = cols // PAIR
    piece = w // outer
    f32, bf16 = jnp.float32, jnp.bfloat16
    dma = pltpu.SemaphoreType.DMA
    vmem = pl.BlockSpec(memory_space=pltpu.VMEM)
    hbm = pl.BlockSpec(memory_space=pl.ANY)
    task = (blocks, CHUNKS, orbitals)
    line = task + (max(outer - 1, 1),)
    green, sigma = pl.pallas_call(
        functools.partial(window_kernel, moms, shards, CHUNKS),
        out_shape=(
            jax.ShapeDtypeStruct((orbitals, 2, rows, cols), f32),
            jax.ShapeDtypeStruct((orbitals, 2, rows, cols), f32),
        ),
        in_specs=[hbm, hbm, vmem],
        out_specs=(vmem, vmem),
        scratch_shapes=[
            pltpu.VMEM((orbitals, 2, hist_rows, cols), f32),
            pltpu.VMEM((orbitals, 2, hist_rows + new_rows, cols), bf16),
            pltpu.VMEM((orbitals, 2, hist_rows + new_rows, cols), bf16),
            pltpu.VMEM((blocks, orbitals, 2, rows, cols), f32),
            pltpu.VMEM(task + (2, w, half), f32),
            pltpu.VMEM((blocks, orbitals, 2, rows, half), f32),
            pltpu.VMEM(line + (2, piece, half), f32),
            pltpu.VMEM((blocks + 1, orbitals, shards, 2, rows, cols), f32),
            pltpu.VMEM((2, w, cols), f32),
            pltpu.VMEM((blocks, comps, rows, 1), f32),
            dma((1 + orbitals,)),
            dma(task), dma(task),
            dma(line), dma(line), dma(line), dma(line),
            dma(task), dma(task),
            dma(task + (shards,)), dma(task + (shards,)),
            dma(task + (shards,)), dma(task + (shards,)),
        ],
        compiler_params=pltpu.CompilerParams(
            collective_id=0, has_side_effects=True, vmem_limit_bytes=56 * 1024 * 1024
        ),
    )(
        history.reshape(orbitals, 2, hist_rows, cols),
        sigma_first.reshape(orbitals, 2, rows, cols),
        propagator.reshape(comps, new_rows),
    )
    return green.reshape(comps, 1, rows, cols), sigma.reshape(comps, rows, cols)


def body(history, sigma_first, propagator):
    moms, shards = lax.axis_size("mom"), lax.axis_size("tm")
    rows = sigma_first.shape[1]
    tiled = moms % PAIR == 0 and rows % (CHUNKS * (moms // PAIR) * SUBLANES) == 0
    tiled = tiled and shards % PAIR == 0 and history.shape[3] % (PAIR * LANES) == 0
    tiled = tiled and rows % LANES == 0 and history.shape[2] % LANES == 0
    whole = history.shape[2] + propagator.shape[2] == history.shape[3] * shards
    if history.shape[1] == 1 and tiled and whole:
        return kernel_body(moms, shards, history, sigma_first, propagator)
    return plain_body(history, sigma_first, propagator)


def solution(mesh):
    placed = (P(None, "mom", None, "tm"), P(None, None, "tm"), P(None, "mom", None))
    return jax.shard_map(
        body,
        mesh=mesh,
        in_specs=placed,
        out_specs=(P(None, "mom", None, "tm"), P(None, None, "tm")),
        check_vma=False,
    )
```

time: 360 us -> 87.3 us (0.24)
  waiting for transfers between devices: 278 us -> 0 us
  Pallas kernels: 0 us -> 81.4 us
  matrix products: 45.4 us -> 0 us
  between operations: 14.5 us -> 0.64 us
  other arithmetic: 12.2 us -> 0 us
    psum x3 -> x0, waiting for transfers between devices: 217 us -> none  [body(): local = lax.psum(partial_sum, 'mom') * norm_factor]
    pallas_call x0 -> x1, Pallas kernels: none -> 81.4 us  [kernel_body(): pl.pallas_call(functools.partial(window_kernel, moms, shards, CHUNKS), ou...]
    all_gather x3 -> x0, waiting for transfers between devices: 59.8 us -> none  [the longest x2 39 us: body(): sigma_full = lax.all_gather(sigma_cols, 'tm', axis=2, tiled=True)]
    dot_general x24 -> x0, matrix products: 45.4 us -> none  [the longest x6 12.6 us: contract(): jnp.einsum('tu,kus->kts', s_re, h_im, precision=hp)]
    mul x11 -> x0, other arithmetic: 8.14 us -> none  [the longest x3 3.26 us: body(): local = lax.psum(partial_sum, 'mom') * norm_factor]
  transfers between devices with their start and end apart: 6 -> 0, of which waited for: 6 -> 0; matrix products, arithmetic and copies ran while one was open for 3% -> 0% of each run, Pallas kernels for 0% -> 0%
where the time goes in v2:
time: 87.3 us; the launch traced here: 87 us
  Pallas kernels  81.4 us (93%)
  local copies, waits for them, and re-layouts  5.02 us (6%)
    pallas_call x1, Pallas kernels, kernel_body(): pl.pallas_call(functools.partial(window_kernel, moms, shards, CHUNKS), ou...  81.4 us
    unnamed x3, local copies, waits for them, and re-layouts  5.02 us

profile of v2, /device:TPU:0, one launch (start us, length us, event | category | flops | bytes accessed | tf_op | source)
XLA Modules:
  0.0 87.0 jit_solution(4776276895909431745)
XLA Ops:
  0.6 1.3 %copy.8 = f32[4,1,384]{2,0,1:T(4,128)} copy(f32[4,1,384]{2,1,0:T(1,128)} %param.5) | data formatting | bytes 12288
  1.9 81.4 %shard_map.50 = (f32[2,2,128,256]{3,2,1,0:T(8,128)}, f32[2,2,128,256]{3,2,1,0:T(8,128)}) custom-call(f32[2,2,640,256]{3,2,1,0:T(8,128)} %bitcast.9, f32[2,2,128,256]{3,2,1,0:T(8,128)} %bitcast.12, f32[4,384]{1,0:T(4,128)} %bitcast.13), custom_call_target="tpu_custom_call" | custom-call | tf_op jit(solution)/shard_map/pallas_call | solution.py:406
  83.3 1.9 %copy.11 = f32[4,1,128,256]{3,2,1,0:T(8,128)} copy(f32[4,1,128,256]{3,2,1,0:T(8,128)} %bitcast.11) | data formatting | bytes 1048576
  85.2 1.9 %copy.12 = f32[4,128,256]{2,1,0:T(8,128)} copy(f32[4,128,256]{2,1,0:T(8,128)} %bitcast.10) | data formatting | bytes 1048576

commit v3 on v2

--- a/solution.py
+++ b/solution.py
@@ -125,7 +125,7 @@
 ):
     orbitals, _, hist_rows, cols = hist_ref.shape
     rows = sig_ref.shape[2]
-    blocks = prop_ref.shape[1] // rows
+    blocks = prop_ref.shape[2] // rows
     outer = moms // PAIR
     w = rows // chunks
     half = cols // PAIR
@@ -246,7 +246,7 @@
     diagonal = square == lax.broadcasted_iota(jnp.int32, (rows, rows), 1)
     for b in range(blocks):
         for c in range(2 * orbitals):
-            line = prop_ref[c : c + 1, b * rows : (b + 1) * rows]
+            line = prop_ref[c, :, b * rows : (b + 1) * rows]
             pcol[b, c] = jnp.sum(jnp.where(diagonal, line, 0.0), axis=1, keepdims=True)
     gh[:, :, hist_rows:] = jnp.zeros((orbitals, 2, blocks * rows, cols), jnp.bfloat16)
     gl[:, :, hist_rows:] = jnp.zeros((orbitals, 2, blocks * rows, cols), jnp.bfloat16)
@@ -385,6 +385,11 @@
                 for d in range(1, outer):
                     line_sum(b, r, o, d).wait_send()
                     line_copy(b, r, o, d).wait_send()
+
+
+def deliver(green_ref, sigma_ref, green_out, sigma_out):
+    green_out[...] = green_ref[...]
+    sigma_out[...] = sigma_ref[...]
 
 
 def kernel_body(moms, shards, history, sigma_first, propagator):
@@ -435,8 +440,17 @@
     )(
         history.reshape(orbitals, 2, hist_rows, cols),
         sigma_first.reshape(orbitals, 2, rows, cols),
-        propagator.reshape(comps, new_rows),
+        propagator,
     )
+    green, sigma = pl.pallas_call(
+        deliver,
+        out_shape=(
+            jax.ShapeDtypeStruct((orbitals, 2, rows, cols), f32),
+            jax.ShapeDtypeStruct((orbitals, 2, rows, cols), f32),
+        ),
+        in_specs=[vmem, vmem],
+        out_specs=(vmem, vmem),
+    )(green, sigma)
     return green.reshape(comps, 1, rows, cols), sigma.reshape(comps, rows, cols)
 
 

time: 87.3 us -> 84.4 us (0.967)
  local copies, waits for them, and re-layouts: 5.02 us -> 0 us
  Pallas kernels: 81.4 us -> 83.6 us
    unnamed x3 -> x0, local copies, waits for them, and re-layouts: 5.02 us -> none
    pallas_call x0 -> x1, Pallas kernels: none -> 2.2 us  [kernel_body(): pl.pallas_call(deliver, out_shape=(jax.ShapeDtypeStruct((orbitals, 2, row...]
where the time goes in v3:
time: 84.4 us; the launch traced here: 84.2 us
  Pallas kernels  83.6 us (99%)
    pallas_call x1, Pallas kernels, kernel_body(): pl.pallas_call(functools.partial(window_kernel, moms, shards, CHUNKS), ou...  81.4 us
    pallas_call x1, Pallas kernels, kernel_body(): pl.pallas_call(deliver, out_shape=(jax.ShapeDtypeStruct((orbitals, 2, row...  2.2 us

profile of v3, /device:TPU:0, one launch (start us, length us, event | category | flops | bytes accessed | tf_op | source)
XLA Modules:
  0.0 84.2 jit_solution(13107974417428776003)
XLA Ops:
  0.6 81.4 %shard_map.50 = (f32[2,2,128,256]{3,2,1,0:T(8,128)}, f32[2,2,128,256]{3,2,1,0:T(8,128)}) custom-call(f32[2,2,640,256]{3,2,1,0:T(8,128)} %bitcast.6, f32[2,2,128,256]{3,2,1,0:T(8,128)} %bitcast.7, f32[4,1,384]{2,1,0:T(1,128)} %prop_ref.1), custom_call_target="tpu_custom_call" | custom-call | tf_op jit(solution)/shard_map/pallas_call | solution.py:411
  82.0 2.2 %shard_map.51 = (f32[2,2,128,256]{3,2,1,0:T(8,128)}, f32[2,2,128,256]{3,2,1,0:T(8,128)}) custom-call(f32[2,2,128,256]{3,2,1,0:T(8,128)} %get-tuple-element.6.green_ref, f32[2,2,128,256]{3,2,1,0:T(8,128)} %get-tuple-element.7.sigma_ref), custom_call_target="tpu_custom_call" | custom-call | tf_op jit(solution)/shard_map/pallas_call | solution.py:445

commit v4 on v3

--- a/solution.py
+++ b/solution.py
@@ -98,7 +98,7 @@
 
 
 def stage_order(blocks, tasks, last_stage):
-    lag = (3.0, 4.0, 4.0, 3.0, 3.0, 1.5)
+    lag = (1.5, 2.0, 2.0, 1.5, 1.5, 0.75)
     busy = (1.0, 0.2, 0.2, 0.1, 0.1, 0.1)
     ready = [(0.0, 0, task, 0) for task in range(tasks)]
     now, order = 0.0, []

time: 84.4 us -> 86.4 us (1.024)
  Pallas kernels: 83.6 us -> 85.6 us
    pallas_call x1, Pallas kernels: 81.4 us -> 83.4 us  [kernel_body(): pl.pallas_call(functools.partial(window_kernel, moms, shards, CHUNKS), ou...]
where the time goes in v4:
time: 86.4 us; the launch traced here: 86.2 us
  Pallas kernels  85.6 us (99%)
    pallas_call x1, Pallas kernels, kernel_body(): pl.pallas_call(functools.partial(window_kernel, moms, shards, CHUNKS), ou...  83.4 us
    pallas_call x1, Pallas kernels, kernel_body(): pl.pallas_call(deliver, out_shape=(jax.ShapeDtypeStruct((orbitals, 2, row...  2.2 us

profile of v4, /device:TPU:0, one launch (start us, length us, event | category | flops | bytes accessed | tf_op | source)
XLA Modules:
  0.0 86.2 jit_solution(4665150156651559250)
XLA Ops:
  0.6 83.4 %shard_map.50 = (f32[2,2,128,256]{3,2,1,0:T(8,128)}, f32[2,2,128,256]{3,2,1,0:T(8,128)}) custom-call(f32[2,2,640,256]{3,2,1,0:T(8,128)} %bitcast.6, f32[2,2,128,256]{3,2,1,0:T(8,128)} %bitcast.7, f32[4,1,384]{2,1,0:T(1,128)} %prop_ref.1), custom_call_target="tpu_custom_call" | custom-call | tf_op jit(solution)/shard_map/pallas_call | solution.py:411
  84.0 2.2 %shard_map.51 = (f32[2,2,128,256]{3,2,1,0:T(8,128)}, f32[2,2,128,256]{3,2,1,0:T(8,128)}) custom-call(f32[2,2,128,256]{3,2,1,0:T(8,128)} %get-tuple-element.6.green_ref, f32[2,2,128,256]{3,2,1,0:T(8,128)} %get-tuple-element.7.sigma_ref), custom_call_target="tpu_custom_call" | custom-call | tf_op jit(solution)/shard_map/pallas_call | solution.py:445
